TPU v7x, 256 devices: a whole 4x4x8 slice. The times are simulated.
256 devices in a mesh: pole: 4 (over y), row: 8 (over z_lo, x), col: 8 (over z_hi, core).
Axes of the slice: x: 4, y: 4, z: 8 (z_hi: 4, z_lo: 2; z = z_hi * 2 + z_lo), core: 2. Of those that a mesh axis runs over, the one named last changes fastest.
Arguments:
- found_inverse: bfloat16 [4, 2, 8192, 8, 8, 128], P('pole', None, 'row', None, 'col'), may hold values from -0.125 to 0.125
- l_panel: bfloat16 [4, 2, 8192, 512], P('pole', None, ('row', 'col')), may hold values from -1.5 to 1.5
- block_pattern: int32 [64, 4], P(('row', 'col')), may hold values 0 or 1
- sup_widths: int32 [4], replicated, may hold values from 1 to 128, 320 in all
- diag_inverse: bfloat16 [4, 2, 512, 128], P('pole'), may hold values from -6 to 6
- pole_weights: float32 [4, 2], P('pole'), may hold values from -4 to 4
Outputs:
- density: float32 [512, 8192], P('col', 'row')
- diagonal: float32 [512, 128], replicated
Inputs may be any that keep to these rules, and one draw needn't show every extreme that they name: `sup_widths`: one supernode has exactly 128 columns.
All inputs are finite; a program needn't handle non-finite values. No bound on the sum of `block_pattern` on one device may be relied on, other than what follows from the above.
Results may differ from a plain program's by a relative error of at most 0.0003.
Values may be sent and summed in bfloat16 or wider, within the bound.
A program may use at most 128 MiB of HBM per device.

v0:
```python
import jax
import jax.numpy as jnp
from jax import lax
from jax.sharding import PartitionSpec as P


def contract(left, right):
    return jnp.einsum("jk,ij->ki", left, right, preferred_element_type=jnp.float32)


def pair_product(left, right):
    return jnp.einsum("ika,kbi->kab", left, right, precision=lax.Precision.HIGHEST)


def per_device(found_inverse, l_panel, block_pattern, sup_widths, diag_inverse, pole_weights):
    slot_width = diag_inverse.shape[-1]
    total_cols = l_panel.shape[-1]
    supernodes = total_cols // slot_width
    row_count = lax.axis_size("row")
    col_count = lax.axis_size("col")
    row_index = lax.axis_index("row")
    col_index = lax.axis_index("col")
    columns = jnp.arange(total_cols, dtype=jnp.int32)
    column_ok = columns % slot_width < jnp.repeat(sup_widths, slot_width)
    block_ok = jnp.repeat(block_pattern[0], slot_width) == 1
    masked = jnp.where(
        (column_ok & block_ok)[None, None, :], l_panel[0], jnp.zeros((), jnp.bfloat16)
    )
    everything = lax.all_gather(masked, ("row", "col"), axis=1, tiled=True)
    own_rows = lax.dynamic_slice_in_dim(
        everything, row_index * col_count * slot_width, col_count * slot_width, 1
    )
    grouped = everything.reshape(2, row_count, col_count, slot_width, total_cols)
    picked = lax.dynamic_index_in_dim(grouped, col_index, 2, keepdims=False)
    column_rows = picked.reshape(2, row_count * slot_width, total_cols)
    local_rows = found_inverse.shape[2]
    inverse = found_inverse[0].reshape(2, local_rows, row_count * slot_width)
    part_real = contract(column_rows[1], inverse[1]) - contract(column_rows[0], inverse[0])
    part_imag = -(contract(column_rows[1], inverse[0]) + contract(column_rows[0], inverse[1]))
    w_real = pole_weights[0, 0]
    w_imag = pole_weights[0, 1]
    weighted = w_real * part_real - w_imag * part_imag
    whole = lax.psum(weighted, "pole")
    density = lax.psum_scatter(whole, "col", scatter_dimension=0, tiled=True)
    lifted = own_rows.astype(jnp.float32).reshape(2, local_rows, supernodes, slot_width)
    upper_real = part_real.reshape(supernodes, slot_width, local_rows)
    upper_imag = part_imag.reshape(supernodes, slot_width, local_rows)
    t_real = pair_product(lifted[0], upper_real) - pair_product(lifted[1], upper_imag)
    t_imag = pair_product(lifted[0], upper_imag) + pair_product(lifted[1], upper_real)
    lead_flag = ((row_index == 0) & (col_index == 0)).astype(jnp.float32)
    d_real = diag_inverse[0, 0].astype(jnp.float32).reshape(supernodes, slot_width, slot_width)
    d_imag = diag_inverse[0, 1].astype(jnp.float32).reshape(supernodes, slot_width, slot_width)
    local_term = lead_flag * (w_real * d_real - w_imag * d_imag) - (
        w_real * t_real - w_imag * t_imag
    )
    diagonal = lax.psum(local_term.reshape(total_cols, slot_width), ("pole", "row", "col"))
    return (density, diagonal)


def solution(mesh):
    in_specs = (
        P("pole", None, "row", None, "col", None),
        P("pole", None, ("row", "col"), None),
        P(("row", "col"), None),
        P(),
        P("pole", None, None, None),
        P("pole", None),
    )
    out_specs = (P("col", "row"), P())
    return jax.shard_map(
        per_device, mesh=mesh, in_specs=in_specs, out_specs=out_specs, check_vma=False
    )
```

profile of v0, /device:TPU:1, one launch (start us, length us, event | category | flops | bytes accessed | tf_op | source)
XLA Modules:
  0.0 512.9 jit_solution(14721515015720495059)
XLA Ops:
  7.9 0.7 fusion.25
  8.6 1.7 bitcast_select_fusion
  10.4 1.3 fusion.27
  11.7 3.8 fusion.26
  15.5 129.0 %all-gather.2.cloned.1.call-done = bf16[2,8192,512]{2,1,0:T(8,128)(2,1)} async-done(((bf16[2,128,512]{2,1,0:T(8,128)(2,1)}), bf16[2,8192,512]{2,1,0:T(8,128)(2,1)}) %all-gather.2.cloned.1.call-update) | async-done | bytes 16777232 | tf_op jit(solution)/shard_map/all_gather | solution.py:29
  144.5 1.7 constant_dynamic-slice_fusion.3
  146.3 1.3 fusion
  147.6 1.3 fusion.2
  149.2 1.3 fusion.12
  150.5 4.6 multiply_subtract_fusion
  155.1 0.9 copy-done.3
  156.0 1.3 subtract_multiply_fusion
  157.3 3.0 constant_dynamic-slice_fusion.2
  160.3 1.5 copy.9
  161.8 2.3 copy.8
  164.0 3.3 fusion.29
  167.3 1.2 fusion.28
  168.9 1.9 fusion.20
  170.8 2.5 fusion.19
  173.3 22.1 %reduce-scatter.2.cloned.1.call-done = f32[64,1024]{1,0:T(8,128)} async-done(((f32[512,1024]{1,0:T(8,128)}), f32[64,1024]{1,0:T(8,128)}) %reduce-scatter.2.cloned.1.call-update) | async-done | bytes 262160 | tf_op jit(solution)/shard_map/reduce_scatter | solution.py:44
  195.5 260.1 %all-reduce.3.cloned.1.call-done = f32[512,128]{1,0:T(8,128)} async-done(((f32[512,128]{1,0:T(8,128)}), f32[512,128]{1,0:T(8,128)}) %all-reduce.3.cloned.1.call-update) | async-done | bytes 262160 | tf_op jit(solution)/shard_map/psum | solution.py:56
  455.6 47.4 %all-reduce.5.cloned.1.call-done = f32[64,1024]{1,0:T(8,128)} async-done(((f32[64,1024]{1,0:T(8,128)}), f32[64,1024]{1,0:T(8,128)}) %all-reduce.5.cloned.1.call-update) | async-done | bytes 262160 | tf_op jit(solution)/shard_map/psum | solution.py:43
  503.0 1.7 copy.36
  504.7 1.7 copy.37
  (16 shorter events, 1.5 us)
Async XLA Ops:
  7.2 137.3 %all-gather.2.cloned.1.call-start = ((), (), s32[]{:S(2)}) async-start(), calls=%async_computation.1 | async-start | bytes 17039360 | tf_op jit(solution)/shard_map/all_gather | solution.py:29
  10.3 185.1 %reduce-scatter.2.cloned.1.call-start = ((), (), s32[]{:S(2)}) async-start(), calls=%async_computation.3 | async-start | bytes 2359296 | tf_op jit(solution)/shard_map/reduce_scatter | solution.py:44
  147.6 1.6 copy-start.2
  155.0 0.9 copy-start.3
  155.1 300.5 %all-reduce.3.cloned.1.call-start = ((), (), s32[]{:S(2)}) async-start(), calls=%async_computation.2 | async-start | bytes 524288 | tf_op jit(solution)/shard_map/psum | solution.py:56
  164.0 3.3 copy-start.1
  167.3 1.6 copy-start
  173.3 329.8 %all-reduce.5.cloned.1.call-start = ((), (), s32[]{:S(2)}) async-start(), calls=%async_computation.4 | async-start | bytes 524288 | tf_op jit(solution)/shard_map/psum | solution.py:43
Sparse Core Ops, SparseCore 0:
  10.4 134.0 all-gather.1
  155.2 40.1 reduce-scatter.1
  201.5 254.0 all-reduce.2
  457.8 45.1 all-reduce.4
where the time goes:
time: 515 us; the launch traced here: 513 us
  waiting for transfers between devices  459 us (89%)
  local copies, waits for them, and re-layouts  18.5 us (4%)
  matrix products  17.3 us (3%)
  between operations  13.9 us (3%)
    psum x1, waiting for transfers between devices, per_device(): lax.psum(local_term.reshape(total_cols, slot_width), ('pole', 'row', 'col'))  260 us
    all_gather x1, waiting for transfers between devices, per_device(): everything = lax.all_gather(masked, ('row', 'col'), axis=1, tiled=True)  129 us
    psum x1, waiting for transfers between devices, per_device(): whole = lax.psum(weighted, 'pole')  47.4 us
    reduce_scatter x1, waiting for transfers between devices, per_device(): density = lax.psum_scatter(whole, 'col', scatter_dimension=0, tiled=True)  22.1 us
  transfers between devices with their start and end apart: 4, of which 4 were waited for; matrix products, arithmetic and copies ran while one was open for 4% of the time, Pallas kernels for 0%

commit v1 on v0

--- a/solution.py
+++ b/solution.py
@@ -17,7 +17,6 @@
     total_cols = l_panel.shape[-1]
     supernodes = total_cols // slot_width
     row_count = lax.axis_size("row")
-    col_count = lax.axis_size("col")
     row_index = lax.axis_index("row")
     col_index = lax.axis_index("col")
     columns = jnp.arange(total_cols, dtype=jnp.int32)
@@ -26,13 +25,8 @@
     masked = jnp.where(
         (column_ok & block_ok)[None, None, :], l_panel[0], jnp.zeros((), jnp.bfloat16)
     )
-    everything = lax.all_gather(masked, ("row", "col"), axis=1, tiled=True)
-    own_rows = lax.dynamic_slice_in_dim(
-        everything, row_index * col_count * slot_width, col_count * slot_width, 1
-    )
-    grouped = everything.reshape(2, row_count, col_count, slot_width, total_cols)
-    picked = lax.dynamic_index_in_dim(grouped, col_index, 2, keepdims=False)
-    column_rows = picked.reshape(2, row_count * slot_width, total_cols)
+    column_rows = lax.all_gather(masked, "row", axis=1, tiled=True)
+    own_rows = lax.all_gather(masked, "col", axis=1, tiled=True)
     local_rows = found_inverse.shape[2]
     inverse = found_inverse[0].reshape(2, local_rows, row_count * slot_width)
     part_real = contract(column_rows[1], inverse[1]) - contract(column_rows[0], inverse[0])
@@ -40,8 +34,8 @@
     w_real = pole_weights[0, 0]
     w_imag = pole_weights[0, 1]
     weighted = w_real * part_real - w_imag * part_imag
-    whole = lax.psum(weighted, "pole")
-    density = lax.psum_scatter(whole, "col", scatter_dimension=0, tiled=True)
+    part = lax.psum_scatter(weighted, "col", scatter_dimension=0, tiled=True)
+    density = lax.psum(part, "pole")
     lifted = own_rows.astype(jnp.float32).reshape(2, local_rows, supernodes, slot_width)
     upper_real = part_real.reshape(supernodes, slot_width, local_rows)
     upper_imag = part_imag.reshape(supernodes, slot_width, local_rows)

time: 515 us -> 458 us (0.89)
  waiting for transfers between devices: 459 us -> 405 us
    all_gather x1 -> x2, waiting for transfers between devices: 129 us -> 67.6 us  [the longest x1 36.4 us: per_device(): column_rows = lax.all_gather(masked, 'row', axis=1, tiled=True)]
    reduce_scatter x1, waiting for transfers between devices: 22.1 us -> 29.3 us  [per_device(): part = lax.psum_scatter(weighted, 'col', scatter_dimension=0, tiled=True)]
  transfers between devices with their start and end apart: 4 -> 5, of which waited for: 4 -> 5; matrix products, arithmetic and copies ran while one was open for 4% -> 7% of each run, Pallas kernels for 0% -> 0%
where the time goes in v1:
time: 458 us; the launch traced here: 456 us
  waiting for transfers between devices  405 us (88%)
  matrix products  18 us (4%)
  local copies, waits for them, and re-layouts  15.2 us (3%)
  between operations  13.9 us (3%)
    psum x1, waiting for transfers between devices, per_device(): lax.psum(local_term.reshape(total_cols, slot_width), ('pole', 'row', 'col'))  260 us
    psum x1, waiting for transfers between devices, per_device(): density = lax.psum(part, 'pole')  47.4 us
    all_gather x1, waiting for transfers between devices, per_device(): column_rows = lax.all_gather(masked, 'row', axis=1, tiled=True)  36.4 us
    all_gather x1, waiting for transfers between devices, per_device(): own_rows = lax.all_gather(masked, 'col', axis=1, tiled=True)  31.1 us
    reduce_scatter x1, waiting for transfers between devices, per_device(): part = lax.psum_scatter(weighted, 'col', scatter_dimension=0, tiled=True)  29.3 us
    dot_general x4, matrix products, contract(): jnp.einsum('jk,ij->ki', left, right, preferred_element_type=jnp.float32)  9.91 us
  transfers between devices with their start and end apart: 5, of which 5 were waited for; matrix products, arithmetic and copies ran while one was open for 7% of the time, Pallas kernels for 0%

profile of v1, /device:TPU:1, one launch (start us, length us, event | category | flops | bytes accessed | tf_op | source)
XLA Modules:
  0.0 456.4 jit_solution(11535285280863356408)
XLA Ops:
  7.9 0.7 fusion.25
  8.6 1.7 bitcast_select_fusion
  11.1 1.4 fusion.28
  12.5 3.8 fusion.26
  16.3 36.4 %all-gather.3.cloned.1.call-done = bf16[2,1024,512]{2,1,0:T(8,128)(2,1)} async-done(((bf16[2,128,512]{2,1,0:T(8,128)(2,1)}), bf16[2,1024,512]{2,1,0:T(8,128)(2,1)}) %all-gather.3.cloned.1.call-update) | async-done | bytes 2097168 | tf_op jit(solution)/shard_map/all_gather | solution.py:28
  52.7 2.7 fusion.2
  55.4 1.3 fusion
  57.0 1.3 fusion.12
  58.3 4.6 %multiply_subtract_fusion = (f32[512,1024]{1,0:T(8,128)}, f32[512,1024]{1,0:T(8,128)}) fusion(f32[512,1024]{1,0:T(8,128)S(1)} %fusion.12, f32[]{:T(128)} %bitcast.7, f32[]{:T(128)} %bitcast, f32[512,1024]{1,0:T(8,128)S(1)} %fusion, bf16[128,8,8,128]{3,2,1,0:T(8,128)(2,1)S(1)} %bitcast.67, bf16[2,1024,512]{2,1,0:T(8,128)(2,1)S(1)} %copy-done.3), kind=kOutput, calls=%fused_computation.8 | convolution fusion | flops 1076363264 | bytes 11534344 | tf_op jit(solution)/shard_map/jk,ij->ki/dot_general | solution.py:8
  63.1 0.9 copy-done.4
  63.9 1.3 subtract_multiply_fusion
  65.2 31.1 %all-gather.5.cloned.1.call-done = bf16[2,1024,512]{2,1,0:T(8,128)(2,1)} async-done(((bf16[2,128,512]{2,1,0:T(8,128)(2,1)}), bf16[2,1024,512]{2,1,0:T(8,128)(2,1)}) %all-gather.5.cloned.1.call-update) | async-done | bytes 2097168 | tf_op jit(solution)/shard_map/all_gather | solution.py:29
  96.4 2.7 fusion.27
  99.1 1.3 copy.8
  100.4 1.5 copy.9
  101.9 2.5 fusion.29
  104.5 1.2 fusion.30
  105.7 1.9 fusion.20
  107.5 2.5 fusion.19
  110.1 29.3 %reduce-scatter.2.cloned.1.call-done = f32[64,1024]{1,0:T(8,128)} async-done(((f32[512,1024]{1,0:T(8,128)}), f32[64,1024]{1,0:T(8,128)}) %reduce-scatter.2.cloned.1.call-update) | async-done | bytes 262160 | tf_op jit(solution)/shard_map/reduce_scatter | solution.py:37
  139.4 259.7 %all-reduce.5.cloned.1.call-done = f32[512,128]{1,0:T(8,128)} async-done(((f32[512,128]{1,0:T(8,128)}), f32[512,128]{1,0:T(8,128)}) %all-reduce.5.cloned.1.call-update) | async-done | bytes 262160 | tf_op jit(solution)/shard_map/psum | solution.py:50
  399.1 47.4 %all-reduce.3.cloned.1.call-done = f32[64,1024]{1,0:T(8,128)} async-done(((f32[64,1024]{1,0:T(8,128)}), f32[64,1024]{1,0:T(8,128)}) %all-reduce.3.cloned.1.call-update) | async-done | bytes 262160 | tf_op jit(solution)/shard_map/psum | solution.py:38
  446.5 1.7 copy.36
  448.2 1.7 copy.37
  (20 shorter events, 1.9 us)
Async XLA Ops:
  7.2 45.6 %all-gather.3.cloned.1.call-start = ((), (), s32[]{:S(2)}) async-start(), calls=%async_computation.1 | async-start | bytes 2359296 | tf_op jit(solution)/shard_map/all_gather | solution.py:28
  10.3 86.1 %all-gather.5.cloned.1.call-start = ((), (), s32[]{:S(2)}) async-start(), calls=%async_computation.4 | async-start | bytes 2359296 | tf_op jit(solution)/shard_map/all_gather | solution.py:29
  11.1 128.3 %reduce-scatter.2.cloned.1.call-start = ((), (), s32[]{:S(2)}) async-start(), calls=%async_computation.2 | async-start | bytes 2359296 | tf_op jit(solution)/shard_map/reduce_scatter | solution.py:37
  52.7 2.7 copy-start.3
  55.4 1.6 copy-start.2
  63.0 0.9 copy-start.4
  63.0 336.1 %all-reduce.5.cloned.1.call-start = ((), (), s32[]{:S(2)}) async-start(), calls=%async_computation.5 | async-start | bytes 524288 | tf_op jit(solution)/shard_map/psum | solution.py:50
  101.9 2.6 copy-start
  101.9 2.6 copy-start.1
  110.1 336.4 %all-reduce.3.cloned.1.call-start = ((), (), s32[]{:S(2)}) async-start(), calls=%async_computation.3 | async-start | bytes 524288 | tf_op jit(solution)/shard_map/psum | solution.py:38
Sparse Core Ops, SparseCore 0:
  10.4 42.2 all-gather.2
  55.2 41.1 all-gather.4
  98.9 40.4 reduce-scatter.1
  145.3 253.7 all-reduce.4
  401.2 45.1 all-reduce.2

commit v2 on v1

v2 whole, which is shorter than its diff:
```python
import functools

import jax
import jax.numpy as jnp
from jax import lax
from jax.experimental import pallas as pl
from jax.experimental.pallas import tpu as pltpu
from jax.sharding import PartitionSpec as P

MESH = pl.DeviceIdType.MESH
PACKED = 320
F32, BF16 = jnp.float32, jnp.bfloat16


def nt(left, right):
    return lax.dot_general(left, right, (((1,), (1,)), ((), ())), preferred_element_type=F32)


def nn(left, right):
    return lax.dot_general(left, right, (((1,), (0,)), ((), ())), preferred_element_type=F32)


def split(value):
    high = value.astype(BF16)
    return high, (value - high.astype(F32)).astype(BF16)


NAMES = (
    ["c_z", "c_xp", "c_xm", "c_zxp", "c_zxm", "c_x2", "c_zx2"]
    + ["m_p", "m_m", "m_2", "m_k0", "m_k1", "m_k2", "m_k3"]
    + ["x_core"]
    + [f"x_y{i}" for i in range(3)]
    + [f"x_z{i}" for i in range(3)]
    + [f"x_g{i}" for i in range(7)]
    + ["d_core"]
    + [f"d_r{i}" for i in range(7)]
    + [f"d_y{i}" for i in range(3)]
    + [f"d_z{i}" for i in range(3)]
    + [f"d_a{i}" for i in range(7)]
    + [f"d_g{i}" for i in range(7)]
    + ["c_x2b", "c_zx2b", "m_2b"]
)
INDEX = {name: i for i, name in enumerate(NAMES)}


def kernel(
    sw, bp, pw, lp, dg, g_hbm, dens, diag,
    graw, ga, mc, mr, pmat, accr, acci, xs, xy, bacc, rx, xh, ry, xu, rz, xz, outb,
    dbuf, dr0, d1, drow, d2, dy, d3, dz, dfin, d4,
    gsem, ssem, rsem,
):
    p, r, c = lax.axis_index("pole"), lax.axis_index("row"), lax.axis_index("col")
    x, zl = lax.rem(r, 4), lax.div(r, 4)
    h, k = lax.div(c, 2), lax.rem(c, 2)
    up, down, far = lax.rem(x + 1, 4), lax.rem(x + 3, 4), lax.rem(x + 2, 4)
    other = (1 - zl) * 4
    here = zl * 4
    rp, rm, r2 = here + up, here + down, here + far
    rz0, rzp, rzm, rz2 = other + x, other + up, other + down, other + far
    hp, hm, h2 = lax.rem(h + 1, 4), lax.rem(h + 3, 4), lax.rem(h + 2, 4)
    partner = h * 2 + 1 - k

    rows = []
    for dz_ in range(2):
        for dx in range(4):
            if (dz_, dx) != (0, 0):
                rows.append(lax.rem(zl + dz_, 2) * 4 + lax.rem(x + dx, 4))
    poles = [lax.rem(p + i, 4) for i in range(1, 4)]
    spans = [lax.rem(h + i, 4) for i in range(1, 4)]
    mates = [(p, partner)] + [(q, cc) for q in poles for cc in (c, partner)]

    def copy(name, src, dst, target, arrive=None):
        i = INDEX[name]
        j = INDEX[arrive or name]
        return pltpu.make_async_remote_copy(
            src_ref=src, dst_ref=dst, send_sem=ssem.at[i], recv_sem=rsem.at[j],
            device_id=target, device_id_type=MESH,
        )

    reads = [pltpu.make_async_copy(g_hbm.at[i], graw.at[i], gsem.at[i]) for i in range(2)]
    for read in reads:
        read.start()

    barrier = pltpu.get_barrier_semaphore()
    peers = [(p, rr, c) for rr in rows] + [(p, r, hh * 2 + k) for hh in spans] + [(q, r, cc) for q, cc in mates]
    for peer in peers:
        pl.semaphore_signal(barrier, inc=1, device_id=peer, device_id_type=MESH)

    widths = [sw[i] for i in range(4)]
    starts = [0 * widths[0], widths[0], widths[0] + widths[1], widths[0] + widths[1] + widths[2]]

    def pick(values, which):
        out = jnp.where(which == 0, values[0], values[1])
        out = jnp.where(which == 2, values[2], out)
        return jnp.where(which == 3, values[3], out)

    slot = lax.broadcasted_iota(jnp.int32, (1, 512), 1)
    node, inner = slot // 128, slot % 128
    kept = (inner < pick(widths, node)) & (pick([bp[0, i] for i in range(4)], node) == 1)
    place = jnp.where(kept, pick(starts, node) + inner, -1)
    line = lax.broadcasted_iota(jnp.int32, (PACKED, 512), 0)
    chooser = jnp.where(line == place, 1.0, 0.0).astype(BF16)
    for part in range(2):
        own = nt(chooser, lp[part]).astype(BF16)
        mc[r, part] = own
        mr[c, part] = own

    pl.semaphore_wait(barrier, len(peers))

    mine, own_r = mc.at[r], mr.at[c]
    c_z = copy("c_z", mine, mine, (p, rz0, c))
    c_xp = copy("c_xp", mine, mine, (p, rp, c))
    c_xm = copy("c_xm", mine, mine, (p, rm, c))
    m_p = copy("m_p", own_r, own_r, (p, r, hp * 2 + k))
    m_m = copy("m_m", own_r, own_r, (p, r, hm * 2 + k))
    m_k0 = copy("m_k0", own_r, own_r, (p, r, partner))
    for started in (c_z, c_xp, c_xm, m_p, m_m, m_k0):
        started.start()

    srow = lax.broadcasted_iota(jnp.int32, (512, 1), 0)
    rnode, rinner = srow // 128, srow % 128
    rplace = jnp.where(rinner < pick(widths, rnode), pick(starts, rnode) + rinner, -1)
    across = lax.broadcasted_iota(jnp.int32, (512, PACKED), 1)
    pmat[...] = jnp.where(across == rplace, 1.0, 0.0).astype(BF16)

    def relayout(part):
        reads[part].wait()

        @pl.loop(0, 32)
        def _(i):
            at = pl.multiple_of(i * 32, 32)
            block = graw[part, pl.ds(at, 32)]
            turned = jnp.swapaxes(block.astype(F32), 0, 1).astype(BF16)
            ga[:, pl.ds(at, 32), part * 128 : part * 128 + 128] = turned

    relayout(0)

    c_xp.wait_recv()
    c_x2 = copy("c_x2", mc.at[rm, 0], mc.at[rm, 0], (p, rp, c))
    c_x2.start()
    c_xm.wait_recv()
    c_x2b = copy("c_x2b", mc.at[rp, 1], mc.at[rp, 1], (p, rm, c), "c_x2")
    c_x2b.start()
    c_z.wait_recv()
    c_zxp = copy("c_zxp", mc.at[rz0], mc.at[rz0], (p, rp, c))
    c_zxm = copy("c_zxm", mc.at[rz0], mc.at[rz0], (p, rm, c))
    c_zxp.start()
    c_zxm.start()

    relayout(1)

    accr[...] = jnp.zeros_like(accr)
    acci[...] = jnp.zeros_like(acci)

    def multiply(a):
        real, imag = mc[a, 0], mc[a, 1]
        right = ga[a]
        accr[...] += nt(jnp.concatenate([real, -imag], axis=1), right)
        acci[...] += nt(jnp.concatenate([imag, real], axis=1), right)

    @pl.loop(0, 4)
    def _(i):
        multiply(jnp.where(i == 0, r, jnp.where(i == 1, rm, jnp.where(i == 2, rp, rz0))))

    c_zxp.wait_recv()
    c_zx2 = copy("c_zx2", mc.at[rzm, 0], mc.at[rzm, 0], (p, rp, c))
    c_zx2.start()
    c_zxm.wait_recv()
    c_zx2b = copy("c_zx2b", mc.at[rzp, 1], mc.at[rzp, 1], (p, rm, c), "c_zx2")
    c_zx2b.start()

    m_p.wait_recv()
    bm, bp_, b2 = hm * 2 + k, hp * 2 + k, h2 * 2 + k
    m_2 = copy("m_2", mr.at[bm, 0], mr.at[bm, 0], (p, r, bp_))
    m_2.start()
    m_k1 = copy("m_k1", mr.at[bm], mr.at[bm], (p, r, partner))
    m_k1.start()
    m_m.wait_recv()
    m_2b = copy("m_2b", mr.at[bp_, 1], mr.at[bp_, 1], (p, r, bm), "m_2")
    m_2b.start()
    m_k2 = copy("m_k2", mr.at[bp_], mr.at[bp_], (p, r, partner))
    m_k2.start()

    copy("c_x2", mc.at[r2], mc.at[r2], (p, rp, c)).wait_recv()

    @pl.loop(0, 3)
    def _(i):
        multiply(jnp.where(i == 0, rzm, jnp.where(i == 1, rzp, r2)))

    copy("c_zx2", mc.at[rz2], mc.at[rz2], (p, rp, c)).wait_recv()
    multiply(rz2)

    w_real, w_imag = pw[0, 0], pw[0, 1]
    for b in range(8):
        lanes = slice(b * 128, b * 128 + 128)
        real, imag = accr[:, lanes], acci[:, lanes]
        xv = w_real * real - w_imag * imag
        yv = w_real * imag + w_imag * real
        xs[b // 4, b % 4] = xv
        xh_, xl_ = split(xv)
        yh_, yl_ = split(yv)
        xy[b] = jnp.concatenate([xh_, yh_, xl_, yl_], axis=1)

    x_core = copy("x_core", xs.at[1 - k], rx, (p, r, partner))
    x_core.start()

    copy("m_2", mr.at[b2], mr.at[b2], (p, r, partner)).wait_recv()
    m_k3 = copy("m_k3", mr.at[b2], mr.at[b2], (p, r, partner))
    m_k3.start()

    x_core.wait_recv()
    for q in range(4):
        xh[q] = xs[k, q] + rx[q]
    x_y = [copy(f"x_y{i}", xh.at[q], ry.at[i], (q, r, c)) for i, q in enumerate(poles)]
    for started in x_y:
        started.start()

    for arrived in (m_k0, m_k1, m_k2, m_k3):
        arrived.wait_recv()
    bacc[...] = jnp.zeros_like(bacc)

    @pl.loop(0, 8)
    def _(b):
        real, imag = mr[b, 0], mr[b, 1]
        left = jnp.concatenate([real, -imag, real, -imag], axis=1)
        bacc[...] += nt(left, xy[b])

    high, low = split(bacc[...])
    tall = nn(pmat[...], high) + nn(pmat[...], low)
    lead = jnp.where((r == 0) & (c == 0), 1.0, 0.0)
    for node_ in range(4):
        band = slice(node_ * 128, node_ * 128 + 128)
        high, low = split(tall[band])
        chosen = pmat[band]
        own_term = w_real * dg[0, band].astype(F32) - w_imag * dg[1, band].astype(F32)
        term = nt(high, chosen) + nt(low, chosen) + lead * own_term
        dbuf[node_ // 2, (node_ % 2) * 2 : (node_ % 2) * 2 + 2] = term.reshape(2, 8, 8, 128)

    d_core = copy("d_core", dbuf.at[1 - k], dr0, (p, r, partner))
    d_core.start()
    d_core.wait_recv()
    d1[...] = dbuf[k] + dr0[...]
    d_r = [copy(f"d_r{i}", d1.at[:, rr], drow.at[i], (p, rr, c)) for i, rr in enumerate(rows)]
    for started in d_r:
        started.start()
    for arrived in d_r:
        arrived.wait_recv()
    d2[...] = d1[:, r] + ((drow[0] + drow[1]) + (drow[2] + drow[3])) + ((drow[4] + drow[5]) + drow[6])
    d_y = [copy(f"d_y{i}", d2.at[q], dy.at[i], (q, r, c)) for i, q in enumerate(poles)]
    for started in d_y:
        started.start()

    for arrived in x_y:
        arrived.wait_recv()
    high, low = split(-((xh[p] + ry[0]) + (ry[1] + ry[2])))
    xu[...] = (nn(pmat[...], high) + nn(pmat[...], low)).reshape(4, 128, 128)

    for arrived in d_y:
        arrived.wait_recv()
    d3[...] = (d2[p] + dy[0]) + (dy[1] + dy[2])
    dz[h] = d3[...]
    d_z = [copy(f"d_z{i}", d3, dz.at[h], (p, r, hh * 2 + k)) for i, hh in enumerate(spans)]
    for started in d_z:
        started.start()
    x_z = [copy(f"x_z{i}", xu.at[hh], rz.at[i], (p, r, hh * 2 + k)) for i, hh in enumerate(spans)]
    for started in x_z:
        started.start()

    for arrived in d_z:
        arrived.wait_recv()
    total = (dz[0] + dz[1]) + (dz[2] + dz[3])
    d4[...] = total
    dfin[k, p, r] = total
    d_a = [copy(f"d_a{i}", d4, dfin.at[k, p, r], (p, rr, c)) for i, rr in enumerate(rows)]
    for started in d_a:
        started.start()

    for arrived in x_z:
        arrived.wait_recv()
    xz[...] = ((xu[h] + rz[0]) + (rz[1] + rz[2])).reshape(2, 64, 128)
    spot = k * 4 + p
    outb[spot] = xz[k]
    x_g = [
        copy(f"x_g{i}", xz.at[lax.rem(cc, 2)], outb.at[spot], (q, r, cc)) for i, (q, cc) in enumerate(mates)
    ]
    for started in x_g:
        started.start()

    for arrived in d_a:
        arrived.wait_recv()
    d_g = [copy(f"d_g{i}", dfin.at[k, p], dfin.at[k, p], (q, r, cc)) for i, (q, cc) in enumerate(mates)]
    for started in d_g:
        started.start()

    for arrived in x_g:
        arrived.wait_recv()
    for b in range(8):
        dens[:, b * 128 : b * 128 + 128] = outb[b]
    for arrived in d_g:
        arrived.wait_recv()
    diag[...] = dfin[...].reshape(512, 128)

    sent = [c_z, c_xp, c_xm, c_x2, c_x2b, c_zxp, c_zxm, c_zx2, c_zx2b, m_p, m_m, m_2, m_2b]
    sent += [m_k0, m_k1, m_k2, m_k3, x_core, d_core]
    sent += x_y + x_z + x_g + d_r + d_y + d_z + d_a + d_g
    for done in sent:
        done.wait_send()


def per_device(found_inverse, l_panel, block_pattern, sup_widths, diag_inverse, pole_weights):
    vmem = pl.BlockSpec(memory_space=pltpu.VMEM)
    smem = pl.BlockSpec(memory_space=pltpu.SMEM)
    n = len(NAMES)
    V = pltpu.VMEM
    return pl.pallas_call(
        kernel,
        out_shape=(jax.ShapeDtypeStruct((64, 1024), F32), jax.ShapeDtypeStruct((512, 128), F32)),
        in_specs=[smem, smem, smem, vmem, vmem, pl.BlockSpec(memory_space=pl.ANY)],
        out_specs=(vmem, vmem),
        scratch_shapes=[
            V((2, 1024, 8, 128), BF16),
            V((8, 1024, 256), BF16),
            V((8, 2, PACKED, 128), BF16),
            V((8, 2, PACKED, 128), BF16),
            V((512, PACKED), BF16),
            V((PACKED, 1024), F32),
            V((PACKED, 1024), F32),
            V((2, 4, PACKED, 128), F32),
            V((8, PACKED, 512), BF16),
            V((PACKED, PACKED), F32),
            V((4, PACKED, 128), F32),
            V((4, PACKED, 128), F32),
            V((3, PACKED, 128), F32),
            V((4, 128, 128), F32),
            V((3, 128, 128), F32),
            V((2, 64, 128), F32),
            V((8, 64, 128), F32),
            V((2, 4, 8, 8, 128), F32),
            V((4, 8, 8, 128), F32),
            V((4, 8, 8, 128), F32),
            V((7, 4, 8, 128), F32),
            V((4, 8, 128), F32),
            V((3, 8, 128), F32),
            V((8, 128), F32),
            V((4, 8, 128), F32),
            V((2, 4, 8, 8, 128), F32),
            V((8, 128), F32),
            pltpu.SemaphoreType.DMA((2,)),
            pltpu.SemaphoreType.DMA((n,)),
            pltpu.SemaphoreType.DMA((n,)),
        ],
        compiler_params=pltpu.CompilerParams(
            collective_id=0, has_side_effects=True, vmem_limit_bytes=48 << 20
        ),
    )(
        sup_widths, block_pattern, pole_weights, l_panel[0], diag_inverse[0],
        found_inverse.reshape(2, 1024, 8, 128),
    )


def solution(mesh):
    in_specs = (
        P("pole", None, "row", None, "col", None),
        P("pole", None, ("row", "col"), None),
        P(("row", "col"), None),
        P(),
        P("pole", None, None, None),
        P("pole", None),
    )
    out_specs = (P("col", "row"), P())
    return jax.shard_map(
        per_device, mesh=mesh, in_specs=in_specs, out_specs=out_specs, check_vma=False
    )
```

time: 458 us -> 68 us (0.15)
  waiting for transfers between devices: 405 us -> 0 us
  Pallas kernels: 0 us -> 59.7 us
  matrix products: 18 us -> 0 us
  between operations: 13.9 us -> 0.65 us
  local copies, waits for them, and re-layouts: 15.2 us -> 7.45 us
    psum x2 -> x0, waiting for transfers between devices: 307 us -> none  [the longest x1 260 us: per_device(): lax.psum(local_term.reshape(total_cols, slot_width), ('pole', 'row', 'col'))]
    all_gather x2 -> x0, waiting for transfers between devices: 67.6 us -> none  [the longest x1 36.4 us: per_device(): column_rows = lax.all_gather(masked, 'row', axis=1, tiled=True)]
    pallas_call x0 -> x1, Pallas kernels: none -> 59.7 us  [per_device(): pl.pallas_call(kernel, out_shape=(jax.ShapeDtypeStruct((64, 1024), F32),...]
    reduce_scatter x1 -> x0, waiting for transfers between devices: 29.3 us -> none  [per_device(): part = lax.psum_scatter(weighted, 'col', scatter_dimension=0, tiled=True)]
    dot_general x8 -> x0, matrix products: 18 us -> none  [the longest x4 9.91 us: contract(): jnp.einsum('jk,ij->ki', left, right, preferred_element_type=jnp.float32)]
    slice x5 -> x0, local copies, waits for them, and re-layouts: 10.7 us -> none  [the longest x2 4.16 us: per_device(): lifted[1]]
  transfers between devices with their start and end apart: 5 -> 0, of which waited for: 5 -> 0; matrix products, arithmetic and copies ran while one was open for 7% -> 0% of each run, Pallas kernels for 0% -> 0%
where the time goes in v2:
time: 68 us; the launch traced here: 67.8 us
  Pallas kernels  59.7 us (88%)
  local copies, waits for them, and re-layouts  7.45 us (11%)
    pallas_call x1, Pallas kernels, per_device(): pl.pallas_call(kernel, out_shape=(jax.ShapeDtypeStruct((64, 1024), F32),...  59.7 us
    unnamed x14, local copies, waits for them, and re-layouts  7.45 us

profile of v2, /device:TPU:1, one launch (start us, length us, event | category | flops | bytes accessed | tf_op | source)
XLA Modules:
  0.0 67.8 jit_solution(8223022709898522152)
XLA Ops:
  0.6 0.0 copy-start
  0.6 2.2 %copy-done = bf16[1,2,1024,8,1,128]{5,3,4,2,1,0:T(8,128)(2,1)S(1)} copy-done((bf16[1,2,1024,8,1,128]{5,3,4,2,1,0:T(8,128)(2,1)S(1)}, bf16[1,2,1024,8,1,128]{5,3,4,2,1,0:T(8,128)(2,1)}, u32[]{:S(2)}) %copy-start) | copy-done | bytes 4194328
  2.8 0.0 copy-start.1
  2.8 0.9 %copy-done.1 = bf16[1,2,128,512]{3,2,1,0:T(8,128)(2,1)S(1)} copy-done((bf16[1,2,128,512]{3,2,1,0:T(8,128)(2,1)S(1)}, bf16[1,2,128,512]{3,2,1,0:T(8,128)(2,1)}, u32[]{:S(2)}) %copy-start.1) | copy-done | bytes 262168
  3.8 0.0 copy-start.2
  3.8 0.9 %copy-done.2 = bf16[1,2,512,128]{3,2,1,0:T(8,128)(2,1)S(1)} copy-done((bf16[1,2,512,128]{3,2,1,0:T(8,128)(2,1)S(1)}, bf16[1,2,512,128]{3,2,1,0:T(8,128)(2,1)}, u32[]{:S(2)}) %copy-start.2) | copy-done | bytes 262168
  4.7 0.0 copy-start.3
  4.7 0.7 copy-done.3
  5.4 0.0 copy-start.4
  5.4 0.7 copy-done.4
  6.0 0.0 copy-start.5
  6.0 0.7 copy-done.5
  6.7 59.7 %shard_map.77 = (f32[64,1024]{1,0:T(8,128)S(1)}, f32[512,128]{1,0:T(8,128)S(1)}) custom-call(s32[4]{0:T(128)S(1)} %copy-done.3, s32[1,4]{1,0:T(1,128)S(1)} %copy-done.4, f32[1,2]{1,0:T(1,128)S(1)} %copy-done.5, bf16[2,128,512]{2,1,0:T(8,128)(2,1)S(1)} %bitcast.4, bf16[2,512,128]{2,1,0:T(8,128)(2,1)S(1)} %bitcast.5, bf16[2,1024,8,128]{3,2,1,0:T(8,128)(2,1)S(1)} %bitcast.3), custom_call_target="tpu_custom_call" | custom-call | tf_op jit(solution)/shard_map/pallas_call | solution.py:315
  66.4 0.7 %copy.10 = f32[64,1024]{1,0:T(8,128)} copy(f32[64,1024]{1,0:T(8,128)S(1)} %get-tuple-element.4) | data formatting | bytes 524288
  67.1 0.7 %copy.11 = f32[512,128]{1,0:T(8,128)} copy(f32[512,128]{1,0:T(8,128)S(1)} %get-tuple-element.5) | data formatting | bytes 524288
Async XLA Ops:
  0.6 2.2 %copy-start = (bf16[1,2,1024,8,1,128]{5,3,4,2,1,0:T(8,128)(2,1)S(1)}, bf16[1,2,1024,8,1,128]{5,3,4,2,1,0:T(8,128)(2,1)}, u32[]{:S(2)}) copy-start(bf16[1,2,1024,8,1,128]{5,3,4,2,1,0:T(8,128)(2,1)} %param.6) | copy-start | bytes 12582916
  2.8 0.9 %copy-start.1 = (bf16[1,2,128,512]{3,2,1,0:T(8,128)(2,1)S(1)}, bf16[1,2,128,512]{3,2,1,0:T(8,128)(2,1)}, u32[]{:S(2)}) copy-start(bf16[1,2,128,512]{3,2,1,0:T(8,128)(2,1)} %param.7) | copy-start | bytes 786436
  3.8 0.9 %copy-start.2 = (bf16[1,2,512,128]{3,2,1,0:T(8,128)(2,1)S(1)}, bf16[1,2,512,128]{3,2,1,0:T(8,128)(2,1)}, u32[]{:S(2)}) copy-start(bf16[1,2,512,128]{3,2,1,0:T(8,128)(2,1)} %param.10) | copy-start | bytes 786436
  4.7 0.7 copy-start.3
  5.4 0.7 copy-start.4
  6.0 0.7 copy-start.5

commit v3 on v2

v3 whole, which is shorter than its diff:
```python
import functools

import jax
import jax.numpy as jnp
from jax import lax
from jax.experimental import pallas as pl
from jax.experimental.pallas import tpu as pltpu
from jax.sharding import PartitionSpec as P

MESH = pl.DeviceIdType.MESH
PACKED = 320
F32, BF16 = jnp.float32, jnp.bfloat16


def nt(left, right):
    return lax.dot_general(left, right, (((1,), (1,)), ((), ())), preferred_element_type=F32)


def nn(left, right):
    return lax.dot_general(left, right, (((1,), (0,)), ((), ())), preferred_element_type=F32)


def split(value):
    high = value.astype(BF16)
    return high, (value - high.astype(F32)).astype(BF16)


HALF = PACKED // 2
NAMES = [
    f"{name}_{half}"
    for half in range(2)
    for name in (
        ["c_z", "c_xp", "c_xm", "c_zxp", "c_zxm", "c_x2", "c_x2b", "c_zx2", "c_zx2b"]
        + [f"c_k{i}" for i in range(8)]
        + [f"x_y{i}" for i in range(3)]
        + [f"x_z{i}" for i in range(3)]
    )
]
NAMES += ["g_0", "g_1", "m_p", "m_m", "m_k"] + [f"x_a{i}" for i in range(4)] + [f"x_b{i}" for i in range(3)]
NAMES += ["d_core"] + [f"d_r{i}" for i in range(7)] + [f"d_y{i}" for i in range(3)]
NAMES += [f"d_z{i}" for i in range(3)] + [f"d_a{i}" for i in range(7)] + [f"d_g{i}" for i in range(7)]
INDEX = {name: i for i, name in enumerate(NAMES)}


def kernel(
    sw_hbm, bp_hbm, pw_hbm, lp_hbm, dg_hbm, g_hbm, dens, diag,
    sw, bp, pw, lp, dg, graw, ga, own, mc, mr, pmat, acc, xs, xy, bacc, ry, xu, rz, xz, outb,
    dbuf, dr0, d1, drow, d2, dy, d3, dz, dfin, d4,
    gsem, ssem, rsem, mssem, mrsem,
):
    p, r, c = lax.axis_index("pole"), lax.axis_index("row"), lax.axis_index("col")
    x, zl = lax.rem(r, 4), lax.div(r, 4)
    h, k = lax.div(c, 2), lax.rem(c, 2)
    up, down, far = lax.rem(x + 1, 4), lax.rem(x + 3, 4), lax.rem(x + 2, 4)
    other = (1 - zl) * 4
    here = zl * 4
    rp, rm, r2 = here + up, here + down, here + far
    rz0, rzp, rzm, rz2 = other + x, other + up, other + down, other + far
    hp, hm = lax.rem(h + 1, 4), lax.rem(h + 3, 4)
    partner = h * 2 + 1 - k
    side = lax.div(h, 2)

    rows = []
    for dz_ in range(2):
        for dx in range(4):
            if (dz_, dx) != (0, 0):
                rows.append(lax.rem(zl + dz_, 2) * 4 + lax.rem(x + dx, 4))
    poles = [lax.rem(p + i, 4) for i in range(1, 4)]
    spans = [lax.rem(h + i, 4) for i in range(1, 4)]
    mates = [(p, partner)] + [(q, cc) for q in poles for cc in (c, partner)]

    def copy(name, src, dst, target, arrive=None):
        i = INDEX[name]
        j = INDEX[arrive or name]
        return pltpu.make_async_remote_copy(
            src_ref=src, dst_ref=dst, send_sem=ssem.at[i], recv_sem=rsem.at[j],
            device_id=target, device_id_type=MESH,
        )

    sent = []

    def start(*copies):
        for each in copies:
            each.start()
            sent.append(each)

    small = [
        pltpu.make_async_copy(src, dst, gsem.at[2 + i])
        for i, (src, dst) in enumerate([(sw_hbm, sw), (bp_hbm, bp), (lp_hbm, lp), (pw_hbm, pw), (dg_hbm, dg)])
    ]
    for read in small:
        read.start()
    near = pl.ds(pl.multiple_of(k * 512, 512), 512)
    away = pl.ds(pl.multiple_of((1 - k) * 512, 512), 512)
    reads = [pltpu.make_async_copy(g_hbm.at[i, near], graw.at[k, i], gsem.at[i]) for i in range(2)]
    for read in reads:
        read.start()

    barrier = pltpu.get_barrier_semaphore()
    peers = [(p, rr, c) for rr in rows] + [(p, r, hh * 2 + k) for hh in spans] + [(q, r, cc) for q, cc in mates]
    peers += [(p, r, hh * 2 + 1 - k) for hh in (hp, hm)]
    for peer in peers:
        pl.semaphore_signal(barrier, inc=1, device_id=peer, device_id_type=MESH)

    for read in small[:3]:
        read.wait()
    widths = [sw[i] for i in range(4)]
    starts = [0 * widths[0], widths[0], widths[0] + widths[1], widths[0] + widths[1] + widths[2]]

    def pick(values, which):
        out = jnp.where(which == 0, values[0], values[1])
        out = jnp.where(which == 2, values[2], out)
        return jnp.where(which == 3, values[3], out)

    slot = lax.broadcasted_iota(jnp.int32, (1, 512), 1)
    node, inner = slot // 128, slot % 128
    kept = (inner < pick(widths, node)) & (pick([bp[0, i] for i in range(4)], node) == 1)
    place = jnp.where(kept, pick(starts, node) + inner, -1)
    line = lax.broadcasted_iota(jnp.int32, (PACKED, 512), 0)
    chooser = jnp.where(line == place, 1.0, 0.0).astype(BF16)
    seat = lax.rem(h, 2) * 2 + k
    for part in range(2):
        packed = nt(chooser, lp[part]).astype(BF16)
        own[part] = packed
        for half in range(2):
            mc[half, k, r, part] = packed[half * HALF : half * HALF + HALF]

    @pl.when(side == k)
    def _():
        mr[seat] = own[...]

    pl.semaphore_wait(barrier, len(peers))

    def row(rr):
        return (p, rr, c)

    mate = (p, r, partner)
    for half in range(2):
        mine = mc.at[half, k, r]
        start(
            copy(f"c_z_{half}", mine, mine, row(rz0)),
            copy(f"c_xp_{half}", mine, mine, row(rp)),
            copy(f"c_xm_{half}", mine, mine, row(rm)),
            copy(f"c_k0_{half}", mine, mine, mate),
        )
    start(*[copy(f"g_{i}", g_hbm.at[i, away], graw.at[k, i], mate) for i in range(2)])

    def row_copy(i, target):
        return pltpu.make_async_remote_copy(
            src_ref=own, dst_ref=mr.at[seat], send_sem=ssem.at[INDEX[i]], recv_sem=mrsem.at[seat],
            device_id=(p, r, target), device_id_type=MESH,
        )

    def start_rows():
        start(row_copy("m_p", hp * 2 + side), row_copy("m_m", hm * 2 + side))

        @pl.when(side != k)
        def _():
            row_copy("m_k", partner).start()

    srow = lax.broadcasted_iota(jnp.int32, (512, 1), 0)
    rnode, rinner = srow // 128, srow % 128
    rplace = jnp.where(rinner < pick(widths, rnode), pick(starts, rnode) + rinner, -1)
    across = lax.broadcasted_iota(jnp.int32, (512, PACKED), 1)
    pmat[...] = jnp.where(across == rplace, 1.0, 0.0).astype(BF16)
    acc[...] = jnp.zeros_like(acc)

    def relayout(core, part):
        at = pl.multiple_of((core * 2 + part) * 128, 128)

        @pl.loop(0, 16)
        def _(i):
            band = pl.ds(pl.multiple_of(i * 32, 32), 32)
            block = graw[core, part, band]
            ga[:, band, pl.ds(at, 128)] = jnp.swapaxes(block.astype(F32), 0, 1).astype(BF16)

    for part in range(2):
        reads[part].wait()
        relayout(k, part)

    def arrive(name, half, block):
        ref = mc.at[half, k, block]
        copy(f"{name}_{half}", ref, ref, mate).wait_recv()

    def hand(i, half, block):
        ref = mc.at[half, k, block]
        start(copy(f"c_k{i}_{half}", ref, ref, mate))

    def first(half):
        arrive("c_xp", half, rm)
        ref = mc.at[half, k, rm, 0]
        start(copy(f"c_x2_{half}", ref, ref, row(rp)))
        arrive("c_xm", half, rp)
        ref = mc.at[half, k, rp, 1]
        start(copy(f"c_x2b_{half}", ref, ref, row(rm), f"c_x2_{half}"))
        arrive("c_z", half, rz0)
        ref = mc.at[half, k, rz0]
        start(copy(f"c_zxp_{half}", ref, ref, row(rp)), copy(f"c_zxm_{half}", ref, ref, row(rm)))
        for i, block in ((1, rm), (2, rp), (3, rz0)):
            hand(i, half, block)

    def second(half):
        arrive("c_zxp", half, rzm)
        ref = mc.at[half, k, rzm, 0]
        start(copy(f"c_zx2_{half}", ref, ref, row(rp)))
        arrive("c_zxm", half, rzp)
        ref = mc.at[half, k, rzp, 1]
        start(copy(f"c_zx2b_{half}", ref, ref, row(rm), f"c_zx2_{half}"))
        arrive("c_x2", half, r2)
        for i, block in ((4, rzm), (5, rzp), (6, r2)):
            hand(i, half, block)

    def third(half):
        arrive("c_zx2", half, rz2)
        hand(7, half, rz2)

    def handed(half, which):
        for i, block in which:
            ref = mc.at[half, 1 - k, block]
            copy(f"c_k{i}_{half}", ref, ref, mate).wait_recv()

    def multiply(half, a):
        r0, i0, r1, i1 = mc[half, 0, a, 0], mc[half, 0, a, 1], mc[half, 1, a, 0], mc[half, 1, a, 1]
        right = ga[a]
        acc[half, 0] += nt(jnp.concatenate([r0, -i0, r1, -i1], axis=1), right)
        acc[half, 1] += nt(jnp.concatenate([i0, r0, i1, r1], axis=1), right)

    def early(half):
        handed(half, ((0, r), (1, rm), (2, rp), (3, rz0)))

        @pl.loop(0, 4)
        def _(i):
            multiply(half, jnp.where(i == 0, r, jnp.where(i == 1, rm, jnp.where(i == 2, rp, rz0))))

    def middle(half):
        handed(half, ((4, rzm), (5, rzp), (6, r2)))

        @pl.loop(0, 3)
        def _(i):
            multiply(half, jnp.where(i == 0, rzm, jnp.where(i == 1, rzp, r2)))

    def late(half):
        handed(half, ((7, rz2),))
        multiply(half, rz2)

    def weigh(half):
        w_real, w_imag = pw[0, 0], pw[0, 1]
        for q in range(4):
            lanes = slice(q * 128, q * 128 + 128)
            real, imag = acc[half, 0, :, lanes], acc[half, 1, :, lanes]
            xv = w_real * real - w_imag * imag
            xs[half, q] = xv
        out = [copy(f"x_y{i}_{half}", xs.at[half, q], ry.at[half, i], (q, r, c)) for i, q in enumerate(poles)]
        start(*out)
        for q in range(4):
            lanes = slice(q * 128, q * 128 + 128)
            real, imag = acc[half, 0, :, lanes], acc[half, 1, :, lanes]
            xh_, xl_ = split(w_real * real - w_imag * imag)
            yh_, yl_ = split(w_real * imag + w_imag * real)
            xy[q, half * HALF : half * HALF + HALF] = jnp.concatenate([xh_, yh_, xl_, yl_], axis=1)
        return out

    def seat_wait(s):
        pltpu.make_async_remote_copy(
            src_ref=mr.at[s], dst_ref=mr.at[s], send_sem=mssem.at[s], recv_sem=mrsem.at[s],
            device_id=mate, device_id_type=MESH,
        ).wait_recv()

    def seat_pass(s, part, target):
        return pltpu.make_async_remote_copy(
            src_ref=mr.at[s, part], dst_ref=mr.at[s, part], send_sem=mssem.at[s], recv_sem=mrsem.at[s],
            device_id=(p, r, target * 2 + k), device_id_type=MESH,
        )

    steps = [lax.rem(2 * k + s // 2 - h + 4, 4) for s in range(4)]

    def pass_rows():
        for s in range(4):

            @pl.when(steps[s] == 3)
            def _():
                seat_wait(s)
                seat_pass(s, 0, hp).start()

            @pl.when(steps[s] == 1)
            def _():
                seat_wait(s)
                seat_pass(s, 1, hm).start()

    first(0)
    start_rows()
    for part in range(2):
        copy(f"g_{part}", graw.at[1 - k, part], graw.at[1 - k, part], mate).wait_recv()
        relayout(1 - k, part)
    first(1)
    early(0)
    second(0)
    early(1)
    second(1)
    middle(0)
    third(0)
    for read in small[3:]:
        read.wait()
    pass_rows()
    late(0)
    x_y = [weigh(0)]
    middle(1)
    third(1)
    late(1)
    x_y.append(weigh(1))

    for s in range(4):

        @pl.when((steps[s] == 2) | ((steps[s] == 0) & (s % 2 != k)))
        def _():
            seat_wait(s)

    bacc[...] = jnp.zeros_like(bacc)

    @pl.loop(0, 4)
    def _(b):
        real, imag = mr[b, 0], mr[b, 1]
        left = jnp.concatenate([real, -imag, real, -imag], axis=1)
        bacc[...] += nt(left, xy[b])

    w_real, w_imag = pw[0, 0], pw[0, 1]
    high, low = split(bacc[...])
    tall = nn(pmat[...], high) + nn(pmat[...], low)
    lead = jnp.where((r == 0) & (c == 0), 1.0, 0.0)
    for node_ in range(4):
        band = slice(node_ * 128, node_ * 128 + 128)
        high, low = split(tall[band])
        chosen = pmat[band]
        own_term = w_real * dg[0, band].astype(F32) - w_imag * dg[1, band].astype(F32)
        term = nt(high, chosen) + nt(low, chosen) + lead * own_term
        dbuf[node_ // 2, (node_ % 2) * 2 : (node_ % 2) * 2 + 2] = term.reshape(2, 8, 8, 128)

    d_core = copy("d_core", dbuf.at[1 - k], dr0, mate)
    start(d_core)
    d_core.wait_recv()
    d1[...] = dbuf[k] + dr0[...]
    d_r = [copy(f"d_r{i}", d1.at[:, rr], drow.at[i], row(rr)) for i, rr in enumerate(rows)]
    start(*d_r)

    for arrived in x_y[0] + x_y[1]:
        arrived.wait_recv()
    halves = [-((xs[half, p] + ry[half, 0]) + (ry[half, 1] + ry[half, 2])) for half in range(2)]
    high, low = split(jnp.concatenate(halves, axis=0))
    xu[...] = (nn(pmat[...], high) + nn(pmat[...], low)).reshape(4, 2, 64, 128)
    x_z = []
    for turn, which in enumerate((1 - k, k)):
        x_z.append(
            [
                copy(f"x_z{i}_{turn}", xu.at[hh, which], rz.at[turn, i], (p, r, hh * 2 + k))
                for i, hh in enumerate(spans)
            ]
        )

    for arrived in d_r:
        arrived.wait_recv()
    d2[...] = d1[:, r] + ((drow[0] + drow[1]) + (drow[2] + drow[3])) + ((drow[4] + drow[5]) + drow[6])
    d_y = [copy(f"d_y{i}", d2.at[q], dy.at[i], (q, r, c)) for i, q in enumerate(poles)]
    start(*d_y)
    start(*x_z[0], *x_z[1])

    for arrived in d_y:
        arrived.wait_recv()
    d3[...] = (d2[p] + dy[0]) + (dy[1] + dy[2])
    dz[h] = d3[...]
    d_z = [copy(f"d_z{i}", d3, dz.at[h], (p, r, hh * 2 + k)) for i, hh in enumerate(spans)]
    start(*d_z)

    spot = k * 4 + p
    for arrived in x_z[0]:
        arrived.wait_recv()
    xz[0] = (xu[h, 1 - k] + rz[0, 0]) + (rz[0, 1] + rz[0, 2])
    x_a = [copy(f"x_a{i}", xz.at[0], outb.at[spot], (q, r, partner)) for i, q in enumerate([p] + poles)]
    start(*x_a)

    for arrived in d_z:
        arrived.wait_recv()
    total = (dz[0] + dz[1]) + (dz[2] + dz[3])
    d4[...] = total
    dfin[k, p, r] = total
    d_a = [copy(f"d_a{i}", d4, dfin.at[k, p, r], row(rr)) for i, rr in enumerate(rows)]
    start(*d_a)

    for arrived in x_z[1]:
        arrived.wait_recv()
    xz[1] = (xu[h, k] + rz[1, 0]) + (rz[1, 1] + rz[1, 2])
    outb[spot] = xz[1]
    x_b = [copy(f"x_b{i}", xz.at[1], outb.at[spot], (q, r, c)) for i, q in enumerate(poles)]
    start(*x_b)

    for arrived in d_a:
        arrived.wait_recv()
    d_g = [copy(f"d_g{i}", dfin.at[k, p], dfin.at[k, p], (q, r, cc)) for i, (q, cc) in enumerate(mates)]
    start(*d_g)

    for arrived in x_a + x_b:
        arrived.wait_recv()
    for b in range(8):
        dens[:, b * 128 : b * 128 + 128] = outb[b]
    for arrived in d_g:
        arrived.wait_recv()
    diag[...] = dfin[...].reshape(512, 128)

    for done in sent:
        done.wait_send()

    @pl.when(side != k)
    def _():
        row_copy("m_k", partner).wait_send()

    for s in range(4):

        @pl.when((steps[s] == 3) | (steps[s] == 1))
        def _():
            seat_pass(s, 0, hp).wait_send()


def per_device(found_inverse, l_panel, block_pattern, sup_widths, diag_inverse, pole_weights):
    vmem = pl.BlockSpec(memory_space=pltpu.VMEM)
    n = len(NAMES)
    V = pltpu.VMEM
    return pl.pallas_call(
        kernel,
        out_shape=(jax.ShapeDtypeStruct((64, 1024), F32), jax.ShapeDtypeStruct((512, 128), F32)),
        in_specs=[pl.BlockSpec(memory_space=pltpu.MemorySpace.HBM)] * 6,
        out_specs=(vmem, vmem),
        scratch_shapes=[
            pltpu.SMEM((4,), jnp.int32),
            pltpu.SMEM((1, 4), jnp.int32),
            pltpu.SMEM((1, 2), F32),
            V((2, 128, 512), BF16),
            V((2, 512, 128), BF16),
            V((2, 2, 512, 8, 128), BF16),
            V((8, 512, 512), BF16),
            V((2, PACKED, 128), BF16),
            V((2, 2, 8, 2, HALF, 128), BF16),
            V((4, 2, PACKED, 128), BF16),
            V((512, PACKED), BF16),
            V((2, 2, HALF, 512), F32),
            V((2, 4, HALF, 128), F32),
            V((4, PACKED, 512), BF16),
            V((PACKED, PACKED), F32),
            V((2, 3, HALF, 128), F32),
            V((4, 2, 64, 128), F32),
            V((2, 3, 64, 128), F32),
            V((2, 64, 128), F32),
            V((8, 64, 128), F32),
            V((2, 4, 8, 8, 128), F32),
            V((4, 8, 8, 128), F32),
            V((4, 8, 8, 128), F32),
            V((7, 4, 8, 128), F32),
            V((4, 8, 128), F32),
            V((3, 8, 128), F32),
            V((8, 128), F32),
            V((4, 8, 128), F32),
            V((2, 4, 8, 8, 128), F32),
            V((8, 128), F32),
            pltpu.SemaphoreType.DMA((7,)),
            pltpu.SemaphoreType.DMA((n,)),
            pltpu.SemaphoreType.DMA((n,)),
            pltpu.SemaphoreType.DMA((4,)),
            pltpu.SemaphoreType.DMA((4,)),
        ],
        compiler_params=pltpu.CompilerParams(
            collective_id=0, has_side_effects=True, vmem_limit_bytes=65500000
        ),
    )(
        sup_widths, block_pattern, pole_weights, l_panel[0], diag_inverse[0],
        found_inverse.reshape(2, 1024, 8, 128),
    )


def solution(mesh):
    in_specs = (
        P("pole", None, "row", None, "col", None),
        P("pole", None, ("row", "col"), None),
        P(("row", "col"), None),
        P(),
        P("pole", None, None, None),
        P("pole", None),
    )
    out_specs = (P("col", "row"), P())
    return jax.shard_map(
        per_device, mesh=mesh, in_specs=in_specs, out_specs=out_specs, check_vma=False
    )
```

time: 68 us -> 63.2 us (0.929)
  local copies, waits for them, and re-layouts: 7.45 us -> 3.34 us
    unnamed x14 -> x2, local copies, waits for them, and re-layouts: 7.45 us -> 3.34 us
where the time goes in v3:
time: 63.2 us; the launch traced here: 63.1 us
  Pallas kernels  59.1 us (94%)
  local copies, waits for them, and re-layouts  3.34 us (5%)
  between operations  0.64 us (1%)
    pallas_call x1, Pallas kernels, per_device(): pl.pallas_call(kernel, out_shape=(jax.ShapeDtypeStruct((64, 1024), F32),...  59.1 us
    unnamed x2, local copies, waits for them, and re-layouts  3.34 us

profile of v3, /device:TPU:1, one launch (start us, length us, event | category | flops | bytes accessed | tf_op | source)
XLA Modules:
  0.0 63.1 jit_solution(10642000646792099866)
XLA Ops:
  0.6 59.1 %shard_map.77 = (f32[64,1024]{1,0:T(8,128)}, f32[512,128]{1,0:T(8,128)}) custom-call(s32[4]{0:T(128)} %sw_hbm.1, s32[1,4]{1,0:T(1,128)} %bp_hbm.1, f32[1,2]{1,0:T(1,128)} %pw_hbm.1, bf16[2,128,512]{2,1,0:T(8,128)(2,1)} %bitcast.4, bf16[2,512,128]{2,1,0:T(8,128)(2,1)} %bitcast.5, bf16[2,1024,8,128]{3,2,1,0:T(8,128)(2,1)} %bitcast.3), custom_call_target="tpu_custom_call" | custom-call | tf_op jit(solution)/shard_map/pallas_call | solution.py:426
  59.7 1.7 %copy.10 = f32[64,1024]{1,0:T(8,128)} copy(f32[64,1024]{1,0:T(8,128)} %get-tuple-element.4) | data formatting | bytes 524288
  61.4 1.7 %copy.11 = f32[512,128]{1,0:T(8,128)} copy(f32[512,128]{1,0:T(8,128)} %get-tuple-element.5) | data formatting | bytes 524288

commit v4 on v3

--- a/solution.py
+++ b/solution.py
@@ -37,15 +37,15 @@
     )
 ]
 NAMES += ["g_0", "g_1", "m_p", "m_m", "m_k"] + [f"x_a{i}" for i in range(4)] + [f"x_b{i}" for i in range(3)]
-NAMES += ["d_core"] + [f"d_r{i}" for i in range(7)] + [f"d_y{i}" for i in range(3)]
-NAMES += [f"d_z{i}" for i in range(3)] + [f"d_a{i}" for i in range(7)] + [f"d_g{i}" for i in range(7)]
+NAMES += ["d_core", "d_c"] + [f"d_r{i}" for i in range(7)] + [f"d_s{i}" for i in range(15)]
+NAMES += [f"d_p{i}" for i in range(3)] + [f"d_a{i}" for i in range(7)]
 INDEX = {name: i for i, name in enumerate(NAMES)}
 
 
 def kernel(
     sw_hbm, bp_hbm, pw_hbm, lp_hbm, dg_hbm, g_hbm, dens, diag,
     sw, bp, pw, lp, dg, graw, ga, own, mc, mr, pmat, acc, xs, xy, bacc, ry, xu, rz, xz, outb,
-    dbuf, dr0, d1, drow, d2, dy, d3, dz, dfin, d4,
+    dbuf, dr0, d1, drow, d2, ds, dfin,
     gsem, ssem, rsem, mssem, mrsem,
 ):
     p, r, c = lax.axis_index("pole"), lax.axis_index("row"), lax.axis_index("col")
@@ -97,8 +97,8 @@
         read.start()
 
     barrier = pltpu.get_barrier_semaphore()
-    peers = [(p, rr, c) for rr in rows] + [(p, r, hh * 2 + k) for hh in spans] + [(q, r, cc) for q, cc in mates]
-    peers += [(p, r, hh * 2 + 1 - k) for hh in (hp, hm)]
+    peers = [(p, rr, c) for rr in (rp, rm, rz0)] + [(p, r, hh * 2 + k) for hh in spans]
+    peers += [(q, r, c) for q in poles] + [(p, r, partner)]
     for peer in peers:
         pl.semaphore_signal(barrier, inc=1, device_id=peer, device_id_type=MESH)
 
@@ -226,7 +226,7 @@
         acc[half, 1] += nt(jnp.concatenate([i0, r0, i1, r1], axis=1), right)
 
     def early(half):
-        handed(half, ((0, r), (1, rm), (2, rp), (3, rz0)))
+        handed(half, ((0, r), (1, rm), (2, rp), (3, rz0))[1 - half :])
 
         @pl.loop(0, 4)
         def _(i):
@@ -288,6 +288,7 @@
                 seat_pass(s, 1, hm).start()
 
     first(0)
+    handed(0, ((0, r),))
     start_rows()
     for part in range(2):
         copy(f"g_{part}", graw.at[1 - k, part], graw.at[1 - k, part], mate).wait_recv()
@@ -333,16 +334,29 @@
         chosen = pmat[band]
         own_term = w_real * dg[0, band].astype(F32) - w_imag * dg[1, band].astype(F32)
         term = nt(high, chosen) + nt(low, chosen) + lead * own_term
-        dbuf[node_ // 2, (node_ % 2) * 2 : (node_ % 2) * 2 + 2] = term.reshape(2, 8, 8, 128)
+        dbuf[node_ // 2, (node_ % 2) * 4 : (node_ % 2) * 4 + 4] = term.reshape(4, 4, 8, 128)
 
     d_core = copy("d_core", dbuf.at[1 - k], dr0, mate)
     start(d_core)
     d_core.wait_recv()
     d1[...] = dbuf[k] + dr0[...]
-    d_r = [copy(f"d_r{i}", d1.at[:, rr], drow.at[i], row(rr)) for i, rr in enumerate(rows)]
+    d_r = [copy(f"d_r{i}", d1.at[rr], drow.at[i], row(rr)) for i, rr in enumerate(rows)]
     start(*d_r)
 
-    for arrived in x_y[0] + x_y[1]:
+    for arrived in d_r:
+        arrived.wait_recv()
+    d2[...] = d1[r] + ((drow[0] + drow[1]) + (drow[2] + drow[3])) + ((drow[4] + drow[5]) + drow[6])
+    for arrived in x_y[0]:
+        arrived.wait_recv()
+    seat_d = p * 4 + h
+    ds[seat_d] = d2[p]
+    d_s = [
+        copy(f"d_s{i}", d2.at[q], ds.at[seat_d], (q, r, hh * 2 + k))
+        for i, (q, hh) in enumerate([(q, hh) for q in [p] + poles for hh in [h] + spans][1:])
+    ]
+    start(*d_s)
+
+    for arrived in x_y[1]:
         arrived.wait_recv()
     halves = [-((xs[half, p] + ry[half, 0]) + (ry[half, 1] + ry[half, 2])) for half in range(2)]
     high, low = split(jnp.concatenate(halves, axis=0))
@@ -355,20 +369,17 @@
                 for i, hh in enumerate(spans)
             ]
         )
-
-    for arrived in d_r:
-        arrived.wait_recv()
-    d2[...] = d1[:, r] + ((drow[0] + drow[1]) + (drow[2] + drow[3])) + ((drow[4] + drow[5]) + drow[6])
-    d_y = [copy(f"d_y{i}", d2.at[q], dy.at[i], (q, r, c)) for i, q in enumerate(poles)]
-    start(*d_y)
     start(*x_z[0], *x_z[1])
 
-    for arrived in d_y:
-        arrived.wait_recv()
-    d3[...] = (d2[p] + dy[0]) + (dy[1] + dy[2])
-    dz[h] = d3[...]
-    d_z = [copy(f"d_z{i}", d3, dz.at[h], (p, r, hh * 2 + k)) for i, hh in enumerate(spans)]
-    start(*d_z)
+    for arrived in d_s:
+        arrived.wait_recv()
+    sums = [ds[i] for i in range(16)]
+    while len(sums) > 1:
+        sums = [sums[i] + sums[i + 1] for i in range(0, len(sums), 2)]
+    dfin[k, r, p] = sums[0]
+    piece = dfin.at[k, r, p]
+    d_p = [copy(f"d_p{i}", piece, piece, (q, r, c)) for i, q in enumerate(poles)]
+    start(*d_p)
 
     spot = k * 4 + p
     for arrived in x_z[0]:
@@ -377,12 +388,9 @@
     x_a = [copy(f"x_a{i}", xz.at[0], outb.at[spot], (q, r, partner)) for i, q in enumerate([p] + poles)]
     start(*x_a)
 
-    for arrived in d_z:
-        arrived.wait_recv()
-    total = (dz[0] + dz[1]) + (dz[2] + dz[3])
-    d4[...] = total
-    dfin[k, p, r] = total
-    d_a = [copy(f"d_a{i}", d4, dfin.at[k, p, r], row(rr)) for i, rr in enumerate(rows)]
+    for arrived in d_p:
+        arrived.wait_recv()
+    d_a = [copy(f"d_a{i}", dfin.at[k, r], dfin.at[k, r], row(rr)) for i, rr in enumerate(rows)]
     start(*d_a)
 
     for arrived in x_z[1]:
@@ -394,15 +402,14 @@
 
     for arrived in d_a:
         arrived.wait_recv()
-    d_g = [copy(f"d_g{i}", dfin.at[k, p], dfin.at[k, p], (q, r, cc)) for i, (q, cc) in enumerate(mates)]
-    start(*d_g)
+    d_c = copy("d_c", dfin.at[k], dfin.at[k], mate)
+    start(d_c)
 
     for arrived in x_a + x_b:
         arrived.wait_recv()
     for b in range(8):
         dens[:, b * 128 : b * 128 + 128] = outb[b]
-    for arrived in d_g:
-        arrived.wait_recv()
+    d_c.wait_recv()
     diag[...] = dfin[...].reshape(512, 128)
 
     for done in sent:
@@ -425,7 +432,7 @@
     V = pltpu.VMEM
     return pl.pallas_call(
         kernel,
-        out_shape=(jax.ShapeDtypeStruct((64, 1024), F32), jax.ShapeDtypeStruct((512, 128), F32)),
+        out_shape=(pltpu.VMEM((64, 1024), F32), pltpu.VMEM((512, 128), F32)),
         in_specs=[pl.BlockSpec(memory_space=pltpu.MemorySpace.HBM)] * 6,
         out_specs=(vmem, vmem),
         scratch_shapes=[
@@ -449,16 +456,13 @@
             V((2, 3, 64, 128), F32),
             V((2, 64, 128), F32),
             V((8, 64, 128), F32),
-            V((2, 4, 8, 8, 128), F32),
-            V((4, 8, 8, 128), F32),
-            V((4, 8, 8, 128), F32),
+            V((2, 8, 4, 8, 128), F32),
+            V((8, 4, 8, 128), F32),
+            V((8, 4, 8, 128), F32),
             V((7, 4, 8, 128), F32),
             V((4, 8, 128), F32),
-            V((3, 8, 128), F32),
-            V((8, 128), F32),
-            V((4, 8, 128), F32),
-            V((2, 4, 8, 8, 128), F32),
-            V((8, 128), F32),
+            V((16, 8, 128), F32),
+            V((2, 8, 4, 8, 128), F32),
             pltpu.SemaphoreType.DMA((7,)),
             pltpu.SemaphoreType.DMA((n,)),
             pltpu.SemaphoreType.DMA((n,)),
@@ -466,7 +470,7 @@
             pltpu.SemaphoreType.DMA((4,)),
         ],
         compiler_params=pltpu.CompilerParams(
-            collective_id=0, has_side_effects=True, vmem_limit_bytes=65500000
+            collective_id=0, has_side_effects=True, vmem_limit_bytes=60000000
         ),
     )(
         sup_widths, block_pattern, pole_weights, l_panel[0], diag_inverse[0],

time: 63.2 us -> 58.1 us (0.919)
  Pallas kernels: 59.1 us -> 56 us
  local copies, waits for them, and re-layouts: 3.34 us -> 1.41 us
    pallas_call x1, Pallas kernels: 59.1 us -> 56 us  [per_device(): pl.pallas_call(kernel, out_shape=(pltpu.VMEM((64, 1024), F32), pltpu.VMEM...]
    unnamed x2, local copies, waits for them, and re-layouts: 3.34 us -> 1.41 us
where the time goes in v4:
time: 58.1 us; the launch traced here: 58 us
  Pallas kernels  56 us (96%)
  local copies, waits for them, and re-layouts  1.41 us (2%)
  between operations  0.64 us (1%)
    pallas_call x1, Pallas kernels, per_device(): pl.pallas_call(kernel, out_shape=(pltpu.VMEM((64, 1024), F32), pltpu.VMEM...  56 us
    unnamed x2, local copies, waits for them, and re-layouts  1.41 us

profile of v4, /device:TPU:1, one launch (start us, length us, event | category | flops | bytes accessed | tf_op | source)
XLA Modules:
  0.0 58.0 jit_solution(17049385333968774381)
XLA Ops:
  0.6 56.0 %shard_map.77 = (f32[64,1024]{1,0:T(8,128)S(1)}, f32[512,128]{1,0:T(8,128)S(1)}) custom-call(s32[4]{0:T(128)} %sw_hbm.1, s32[1,4]{1,0:T(1,128)} %bp_hbm.1, f32[1,2]{1,0:T(1,128)} %pw_hbm.1, bf16[2,128,512]{2,1,0:T(8,128)(2,1)} %bitcast.4, bf16[2,512,128]{2,1,0:T(8,128)(2,1)} %bitcast.5, bf16[2,1024,8,128]{3,2,1,0:T(8,128)(2,1)} %bitcast.3), custom_call_target="tpu_custom_call" | custom-call | tf_op jit(solution)/shard_map/pallas_call | solution.py:433
  56.6 0.7 %copy.10 = f32[64,1024]{1,0:T(8,128)} copy(f32[64,1024]{1,0:T(8,128)S(1)} %get-tuple-element.2) | data formatting | bytes 524288
  57.3 0.7 %copy.11 = f32[512,128]{1,0:T(8,128)} copy(f32[512,128]{1,0:T(8,128)S(1)} %get-tuple-element.3) | data formatting | bytes 524288

commit v5 on v4

--- a/solution.py
+++ b/solution.py
@@ -37,15 +37,15 @@
     )
 ]
 NAMES += ["g_0", "g_1", "m_p", "m_m", "m_k"] + [f"x_a{i}" for i in range(4)] + [f"x_b{i}" for i in range(3)]
-NAMES += ["d_core", "d_c"] + [f"d_r{i}" for i in range(7)] + [f"d_s{i}" for i in range(15)]
-NAMES += [f"d_p{i}" for i in range(3)] + [f"d_a{i}" for i in range(7)]
+NAMES += ["d_core", "d_c"] + [f"d_r{i}" for i in range(7)] + [f"d_y{i}" for i in range(3)]
+NAMES += [f"d_z{i}" for i in range(3)] + [f"d_a{i}" for i in range(7)]
 INDEX = {name: i for i, name in enumerate(NAMES)}
 
 
 def kernel(
     sw_hbm, bp_hbm, pw_hbm, lp_hbm, dg_hbm, g_hbm, dens, diag,
     sw, bp, pw, lp, dg, graw, ga, own, mc, mr, pmat, acc, xs, xy, bacc, ry, xu, rz, xz, outb,
-    dbuf, dr0, d1, drow, d2, ds, dfin,
+    dbuf, dr0, d1, drow, d2, dy, d3, dz, dfin,
     gsem, ssem, rsem, mssem, mrsem,
 ):
     p, r, c = lax.axis_index("pole"), lax.axis_index("row"), lax.axis_index("col")
@@ -102,7 +102,7 @@
     for peer in peers:
         pl.semaphore_signal(barrier, inc=1, device_id=peer, device_id_type=MESH)
 
-    for read in small[:3]:
+    for read in small[:2]:
         read.wait()
     widths = [sw[i] for i in range(4)]
     starts = [0 * widths[0], widths[0], widths[0] + widths[1], widths[0] + widths[1] + widths[2]]
@@ -119,6 +119,7 @@
     line = lax.broadcasted_iota(jnp.int32, (PACKED, 512), 0)
     chooser = jnp.where(line == place, 1.0, 0.0).astype(BF16)
     seat = lax.rem(h, 2) * 2 + k
+    small[2].wait()
     for part in range(2):
         packed = nt(chooser, lp[part]).astype(BF16)
         own[part] = packed
@@ -346,16 +347,12 @@
     for arrived in d_r:
         arrived.wait_recv()
     d2[...] = d1[r] + ((drow[0] + drow[1]) + (drow[2] + drow[3])) + ((drow[4] + drow[5]) + drow[6])
+    dy[p] = d2[...]
+    d_y = [copy(f"d_y{i}", d2, dy.at[p], (q, r, c)) for i, q in enumerate(poles)]
+    start(*d_y)
+
     for arrived in x_y[0]:
         arrived.wait_recv()
-    seat_d = p * 4 + h
-    ds[seat_d] = d2[p]
-    d_s = [
-        copy(f"d_s{i}", d2.at[q], ds.at[seat_d], (q, r, hh * 2 + k))
-        for i, (q, hh) in enumerate([(q, hh) for q in [p] + poles for hh in [h] + spans][1:])
-    ]
-    start(*d_s)
-
     for arrived in x_y[1]:
         arrived.wait_recv()
     halves = [-((xs[half, p] + ry[half, 0]) + (ry[half, 1] + ry[half, 2])) for half in range(2)]
@@ -370,16 +367,12 @@
             ]
         )
     start(*x_z[0], *x_z[1])
-
-    for arrived in d_s:
-        arrived.wait_recv()
-    sums = [ds[i] for i in range(16)]
-    while len(sums) > 1:
-        sums = [sums[i] + sums[i + 1] for i in range(0, len(sums), 2)]
-    dfin[k, r, p] = sums[0]
-    piece = dfin.at[k, r, p]
-    d_p = [copy(f"d_p{i}", piece, piece, (q, r, c)) for i, q in enumerate(poles)]
-    start(*d_p)
+    for arrived in d_y:
+        arrived.wait_recv()
+    d3[...] = (dy[0] + dy[1]) + (dy[2] + dy[3])
+    dz[h] = d3[...]
+    d_z = [copy(f"d_z{i}", d3, dz.at[h], (p, r, hh * 2 + k)) for i, hh in enumerate(spans)]
+    start(*d_z)
 
     spot = k * 4 + p
     for arrived in x_z[0]:
@@ -387,11 +380,6 @@
     xz[0] = (xu[h, 1 - k] + rz[0, 0]) + (rz[0, 1] + rz[0, 2])
     x_a = [copy(f"x_a{i}", xz.at[0], outb.at[spot], (q, r, partner)) for i, q in enumerate([p] + poles)]
     start(*x_a)
-
-    for arrived in d_p:
-        arrived.wait_recv()
-    d_a = [copy(f"d_a{i}", dfin.at[k, r], dfin.at[k, r], row(rr)) for i, rr in enumerate(rows)]
-    start(*d_a)
 
     for arrived in x_z[1]:
         arrived.wait_recv()
@@ -400,15 +388,21 @@
     x_b = [copy(f"x_b{i}", xz.at[1], outb.at[spot], (q, r, c)) for i, q in enumerate(poles)]
     start(*x_b)
 
+    for arrived in d_z:
+        arrived.wait_recv()
+    dfin[k, r] = (dz[0] + dz[1]) + (dz[2] + dz[3])
+    d_a = [copy(f"d_a{i}", dfin.at[k, r], dfin.at[k, r], row(rr)) for i, rr in enumerate(rows)]
+    start(*d_a)
+
+    for arrived in x_a + x_b:
+        arrived.wait_recv()
+    for b in range(8):
+        dens[:, b * 128 : b * 128 + 128] = outb[b]
+
     for arrived in d_a:
         arrived.wait_recv()
     d_c = copy("d_c", dfin.at[k], dfin.at[k], mate)
     start(d_c)
-
-    for arrived in x_a + x_b:
-        arrived.wait_recv()
-    for b in range(8):
-        dens[:, b * 128 : b * 128 + 128] = outb[b]
     d_c.wait_recv()
     diag[...] = dfin[...].reshape(512, 128)
 
@@ -461,7 +455,9 @@
             V((8, 4, 8, 128), F32),
             V((7, 4, 8, 128), F32),
             V((4, 8, 128), F32),
-            V((16, 8, 128), F32),
+            V((4, 4, 8, 128), F32),
+            V((4, 8, 128), F32),
+            V((4, 4, 8, 128), F32),
             V((2, 8, 4, 8, 128), F32),
             pltpu.SemaphoreType.DMA((7,)),
             pltpu.SemaphoreType.DMA((n,)),

time: 58.1 us -> 57.8 us (level)
  no operation moved by 1% of the time
where the time goes in v5:
time: 57.8 us; the launch traced here: 57.7 us
  Pallas kernels  55.7 us (96%)
  local copies, waits for them, and re-layouts  1.41 us (2%)
  between operations  0.64 us (1%)
    pallas_call x1, Pallas kernels, per_device(): pl.pallas_call(kernel, out_shape=(pltpu.VMEM((64, 1024), F32), pltpu.VMEM...  55.7 us
    unnamed x2, local copies, waits for them, and re-layouts  1.41 us

profile of v5, /device:TPU:1, one launch (start us, length us, event | category | flops | bytes accessed | tf_op | source)
XLA Modules:
  0.0 57.7 jit_solution(8048383279162769868)
XLA Ops:
  0.6 55.7 %shard_map.77 = (f32[64,1024]{1,0:T(8,128)S(1)}, f32[512,128]{1,0:T(8,128)S(1)}) custom-call(s32[4]{0:T(128)} %sw_hbm.1, s32[1,4]{1,0:T(1,128)} %bp_hbm.1, f32[1,2]{1,0:T(1,128)} %pw_hbm.1, bf16[2,128,512]{2,1,0:T(8,128)(2,1)} %bitcast.4, bf16[2,512,128]{2,1,0:T(8,128)(2,1)} %bitcast.5, bf16[2,1024,8,128]{3,2,1,0:T(8,128)(2,1)} %bitcast.3), custom_call_target="tpu_custom_call" | custom-call | tf_op jit(solution)/shard_map/pallas_call | solution.py:427
  56.3 0.7 %copy.10 = f32[64,1024]{1,0:T(8,128)} copy(f32[64,1024]{1,0:T(8,128)S(1)} %get-tuple-element.2) | data formatting | bytes 524288
  57.0 0.7 %copy.11 = f32[512,128]{1,0:T(8,128)} copy(f32[512,128]{1,0:T(8,128)S(1)} %get-tuple-element.3) | data formatting | bytes 524288

commit v6 on v5

--- a/solution.py
+++ b/solution.py
@@ -36,7 +36,7 @@
         + [f"x_z{i}" for i in range(3)]
     )
 ]
-NAMES += ["g_0", "g_1", "m_p", "m_m", "m_k"] + [f"x_a{i}" for i in range(4)] + [f"x_b{i}" for i in range(3)]
+NAMES += ["c_zx2c", "c_zx2d", "g_0", "g_1", "m_p0", "m_p1", "m_m0", "m_m1", "m_k"] + [f"x_a{i}" for i in range(4)] + [f"x_b{i}" for i in range(3)]
 NAMES += ["d_core", "d_c"] + [f"d_r{i}" for i in range(7)] + [f"d_y{i}" for i in range(3)]
 NAMES += [f"d_z{i}" for i in range(3)] + [f"d_a{i}" for i in range(7)]
 INDEX = {name: i for i, name in enumerate(NAMES)}
@@ -44,9 +44,9 @@
 
 def kernel(
     sw_hbm, bp_hbm, pw_hbm, lp_hbm, dg_hbm, g_hbm, dens, diag,
-    sw, bp, pw, lp, dg, graw, ga, own, mc, mr, pmat, acc, xs, xy, bacc, ry, xu, rz, xz, outb,
+    sw, bp, pw, lp, dg, graw, ga, own, mc, mr, pmat, acc, xs, xy, bacc, dterm, ry, xu, rz, xz, outb,
     dbuf, dr0, d1, drow, d2, dy, d3, dz, dfin,
-    gsem, ssem, rsem, mssem, mrsem,
+    gsem, ssem, rsem, mssem, mrsem, mrest,
 ):
     p, r, c = lax.axis_index("pole"), lax.axis_index("row"), lax.axis_index("col")
     x, zl = lax.rem(r, 4), lax.div(r, 4)
@@ -146,14 +146,25 @@
         )
     start(*[copy(f"g_{i}", g_hbm.at[i, away], graw.at[k, i], mate) for i in range(2)])
 
-    def row_copy(i, target):
+    def row_half(name, part, sem, target):
         return pltpu.make_async_remote_copy(
-            src_ref=own, dst_ref=mr.at[seat], send_sem=ssem.at[INDEX[i]], recv_sem=mrsem.at[seat],
+            src_ref=own.at[part], dst_ref=mr.at[seat, part], send_sem=ssem.at[INDEX[name]], recv_sem=sem.at[seat],
             device_id=(p, r, target), device_id_type=MESH,
         )
 
+    def row_copy(name, target):
+        return pltpu.make_async_remote_copy(
+            src_ref=own, dst_ref=mr.at[seat], send_sem=ssem.at[INDEX[name]], recv_sem=mrsem.at[seat],
+            device_id=(p, r, target), device_id_type=MESH,
+        )
+
     def start_rows():
-        start(row_copy("m_p", hp * 2 + side), row_copy("m_m", hm * 2 + side))
+        start(
+            row_half("m_p0", 0, mrsem, hp * 2 + side),
+            row_half("m_m1", 1, mrsem, hm * 2 + side),
+            row_half("m_p1", 1, mrest, hp * 2 + side),
+            row_half("m_m0", 0, mrest, hm * 2 + side),
+        )
 
         @pl.when(side != k)
         def _():
@@ -188,15 +199,15 @@
         start(copy(f"c_k{i}_{half}", ref, ref, mate))
 
     def first(half):
+        arrive("c_z", half, rz0)
+        ref = mc.at[half, k, rz0]
+        start(copy(f"c_zxp_{half}", ref, ref, row(rp)), copy(f"c_zxm_{half}", ref, ref, row(rm)))
         arrive("c_xp", half, rm)
         ref = mc.at[half, k, rm, 0]
         start(copy(f"c_x2_{half}", ref, ref, row(rp)))
         arrive("c_xm", half, rp)
         ref = mc.at[half, k, rp, 1]
         start(copy(f"c_x2b_{half}", ref, ref, row(rm), f"c_x2_{half}"))
-        arrive("c_z", half, rz0)
-        ref = mc.at[half, k, rz0]
-        start(copy(f"c_zxp_{half}", ref, ref, row(rp)), copy(f"c_zxm_{half}", ref, ref, row(rm)))
         for i, block in ((1, rm), (2, rp), (3, rz0)):
             hand(i, half, block)
 
@@ -204,16 +215,21 @@
         arrive("c_zxp", half, rzm)
         ref = mc.at[half, k, rzm, 0]
         start(copy(f"c_zx2_{half}", ref, ref, row(rp)))
+        if half == 1:
+            start(copy("c_zx2c", ref, ref, (p, rp, partner), "c_k7_1"))
         arrive("c_zxm", half, rzp)
         ref = mc.at[half, k, rzp, 1]
         start(copy(f"c_zx2b_{half}", ref, ref, row(rm), f"c_zx2_{half}"))
+        if half == 1:
+            start(copy("c_zx2d", ref, ref, (p, rm, partner), "c_k7_1"))
         arrive("c_x2", half, r2)
         for i, block in ((4, rzm), (5, rzp), (6, r2)):
             hand(i, half, block)
 
     def third(half):
         arrive("c_zx2", half, rz2)
-        hand(7, half, rz2)
+        if half == 0:
+            hand(7, half, rz2)
 
     def handed(half, which):
         for i, block in which:
@@ -267,6 +283,12 @@
             device_id=mate, device_id_type=MESH,
         ).wait_recv()
 
+    def half_wait(s, part, sem):
+        pltpu.make_async_remote_copy(
+            src_ref=mr.at[s, part], dst_ref=mr.at[s, part], send_sem=mssem.at[s], recv_sem=sem.at[s],
+            device_id=mate, device_id_type=MESH,
+        ).wait_recv()
+
     def seat_pass(s, part, target):
         return pltpu.make_async_remote_copy(
             src_ref=mr.at[s, part], dst_ref=mr.at[s, part], send_sem=mssem.at[s], recv_sem=mrsem.at[s],
@@ -280,12 +302,12 @@
 
             @pl.when(steps[s] == 3)
             def _():
-                seat_wait(s)
+                half_wait(s, 0, mrsem)
                 seat_pass(s, 0, hp).start()
 
             @pl.when(steps[s] == 1)
             def _():
-                seat_wait(s)
+                half_wait(s, 1, mrsem)
                 seat_pass(s, 1, hm).start()
 
     first(0)
@@ -299,11 +321,14 @@
     second(0)
     early(1)
     second(1)
+    pass_rows()
     middle(0)
     third(0)
     for read in small[3:]:
         read.wait()
-    pass_rows()
+    lead = jnp.where((r == 0) & (c == 0), 1.0, 0.0)
+    dterm[...] = (lead * pw[0, 0]) * dg[0].astype(F32) - (lead * pw[0, 1]) * dg[1].astype(F32)
+    bacc[...] = jnp.zeros_like(bacc)
     late(0)
     x_y = [weigh(0)]
     middle(1)
@@ -317,7 +342,13 @@
         def _():
             seat_wait(s)
 
-    bacc[...] = jnp.zeros_like(bacc)
+        @pl.when(steps[s] == 3)
+        def _():
+            half_wait(s, 1, mrest)
+
+        @pl.when(steps[s] == 1)
+        def _():
+            half_wait(s, 0, mrest)
 
     @pl.loop(0, 4)
     def _(b):
@@ -325,16 +356,13 @@
         left = jnp.concatenate([real, -imag, real, -imag], axis=1)
         bacc[...] += nt(left, xy[b])
 
-    w_real, w_imag = pw[0, 0], pw[0, 1]
     high, low = split(bacc[...])
     tall = nn(pmat[...], high) + nn(pmat[...], low)
-    lead = jnp.where((r == 0) & (c == 0), 1.0, 0.0)
     for node_ in range(4):
         band = slice(node_ * 128, node_ * 128 + 128)
         high, low = split(tall[band])
         chosen = pmat[band]
-        own_term = w_real * dg[0, band].astype(F32) - w_imag * dg[1, band].astype(F32)
-        term = nt(high, chosen) + nt(low, chosen) + lead * own_term
+        term = nt(high, chosen) + nt(low, chosen) + dterm[band]
         dbuf[node_ // 2, (node_ % 2) * 4 : (node_ % 2) * 4 + 4] = term.reshape(4, 4, 8, 128)
 
     d_core = copy("d_core", dbuf.at[1 - k], dr0, mate)
@@ -445,6 +473,7 @@
             V((2, 4, HALF, 128), F32),
             V((4, PACKED, 512), BF16),
             V((PACKED, PACKED), F32),
+            V((512, 128), F32),
             V((2, 3, HALF, 128), F32),
             V((4, 2, 64, 128), F32),
             V((2, 3, 64, 128), F32),
@@ -464,6 +493,7 @@
             pltpu.SemaphoreType.DMA((n,)),
             pltpu.SemaphoreType.DMA((4,)),
             pltpu.SemaphoreType.DMA((4,)),
+            pltpu.SemaphoreType.DMA((4,)),
         ],
         compiler_params=pltpu.CompilerParams(
             collective_id=0, has_side_effects=True, vmem_limit_bytes=60000000

time: 57.8 us -> 56.6 us (0.979)
  Pallas kernels: 55.7 us -> 54.5 us
    pallas_call x1, Pallas kernels: 55.7 us -> 54.5 us  [per_device(): pl.pallas_call(kernel, out_shape=(pltpu.VMEM((64, 1024), F32), pltpu.VMEM...]
where the time goes in v6:
time: 56.6 us; the launch traced here: 56.5 us
  Pallas kernels  54.5 us (96%)
  local copies, waits for them, and re-layouts  1.41 us (2%)
  between operations  0.64 us (1%)
    pallas_call x1, Pallas kernels, per_device(): pl.pallas_call(kernel, out_shape=(pltpu.VMEM((64, 1024), F32), pltpu.VMEM...  54.5 us
    unnamed x2, local copies, waits for them, and re-layouts  1.41 us

profile of v6, /device:TPU:1, one launch (start us, length us, event | category | flops | bytes accessed | tf_op | source)
XLA Modules:
  0.0 56.5 jit_solution(11149528538171127362)
XLA Ops:
  0.6 54.5 %shard_map.77 = (f32[64,1024]{1,0:T(8,128)S(1)}, f32[512,128]{1,0:T(8,128)S(1)}) custom-call(s32[4]{0:T(128)} %sw_hbm.1, s32[1,4]{1,0:T(1,128)} %bp_hbm.1, f32[1,2]{1,0:T(1,128)} %pw_hbm.1, bf16[2,128,512]{2,1,0:T(8,128)(2,1)} %bitcast.4, bf16[2,512,128]{2,1,0:T(8,128)(2,1)} %bitcast.5, bf16[2,1024,8,128]{3,2,1,0:T(8,128)(2,1)} %bitcast.3), custom_call_target="tpu_custom_call" | custom-call | tf_op jit(solution)/shard_map/pallas_call | solution.py:455
  55.1 0.7 %copy.10 = f32[64,1024]{1,0:T(8,128)} copy(f32[64,1024]{1,0:T(8,128)S(1)} %get-tuple-element.2) | data formatting | bytes 524288
  55.8 0.7 %copy.11 = f32[512,128]{1,0:T(8,128)} copy(f32[512,128]{1,0:T(8,128)S(1)} %get-tuple-element.3) | data formatting | bytes 524288

commit v7 on v6

--- a/solution.py
+++ b/solution.py
@@ -38,7 +38,7 @@
 ]
 NAMES += ["c_zx2c", "c_zx2d", "g_0", "g_1", "m_p0", "m_p1", "m_m0", "m_m1", "m_k"] + [f"x_a{i}" for i in range(4)] + [f"x_b{i}" for i in range(3)]
 NAMES += ["d_core", "d_c"] + [f"d_r{i}" for i in range(7)] + [f"d_y{i}" for i in range(3)]
-NAMES += [f"d_z{i}" for i in range(3)] + [f"d_a{i}" for i in range(7)]
+NAMES += [f"d_z{i}" for i in range(3)] + [f"d_a{i}" for i in range(7)] + [f"d_b{i}" for i in range(7)]
 INDEX = {name: i for i, name in enumerate(NAMES)}
 
 
@@ -419,19 +419,21 @@
     for arrived in d_z:
         arrived.wait_recv()
     dfin[k, r] = (dz[0] + dz[1]) + (dz[2] + dz[3])
-    d_a = [copy(f"d_a{i}", dfin.at[k, r], dfin.at[k, r], row(rr)) for i, rr in enumerate(rows)]
-    start(*d_a)
+    piece = dfin.at[k, r]
+    d_a = [copy(f"d_a{i}", piece, piece, row(rr)) for i, rr in enumerate(rows)]
+    d_b = [copy(f"d_b{i}", piece, piece, (p, rr, partner)) for i, rr in enumerate(rows)]
+    for pair in zip(d_a, d_b):
+        start(*pair)
+    d_c = copy("d_c", piece, piece, mate)
+    start(d_c)
 
     for arrived in x_a + x_b:
         arrived.wait_recv()
     for b in range(8):
         dens[:, b * 128 : b * 128 + 128] = outb[b]
 
-    for arrived in d_a:
-        arrived.wait_recv()
-    d_c = copy("d_c", dfin.at[k], dfin.at[k], mate)
-    start(d_c)
-    d_c.wait_recv()
+    for arrived in d_a + d_b + [d_c]:
+        arrived.wait_recv()
     diag[...] = dfin[...].reshape(512, 128)
 
     for done in sent:

time: 56.6 us -> 56.3 us (level)
  no operation moved by 1% of the time
where the time goes in v7:
time: 56.3 us; the launch traced here: 56.2 us
  Pallas kernels  54.2 us (96%)
  local copies, waits for them, and re-layouts  1.41 us (3%)
  between operations  0.64 us (1%)
    pallas_call x1, Pallas kernels, per_device(): pl.pallas_call(kernel, out_shape=(pltpu.VMEM((64, 1024), F32), pltpu.VMEM...  54.2 us
    unnamed x2, local copies, waits for them, and re-layouts  1.41 us

profile of v7, /device:TPU:1, one launch (start us, length us, event | category | flops | bytes accessed | tf_op | source)
XLA Modules:
  0.0 56.2 jit_solution(7841399273760624572)
XLA Ops:
  0.6 54.2 %shard_map.77 = (f32[64,1024]{1,0:T(8,128)S(1)}, f32[512,128]{1,0:T(8,128)S(1)}) custom-call(s32[4]{0:T(128)} %sw_hbm.1, s32[1,4]{1,0:T(1,128)} %bp_hbm.1, f32[1,2]{1,0:T(1,128)} %pw_hbm.1, bf16[2,128,512]{2,1,0:T(8,128)(2,1)} %bitcast.4, bf16[2,512,128]{2,1,0:T(8,128)(2,1)} %bitcast.5, bf16[2,1024,8,128]{3,2,1,0:T(8,128)(2,1)} %bitcast.3), custom_call_target="tpu_custom_call" | custom-call | tf_op jit(solution)/shard_map/pallas_call | solution.py:457
  54.8 0.7 %copy.10 = f32[64,1024]{1,0:T(8,128)} copy(f32[64,1024]{1,0:T(8,128)S(1)} %get-tuple-element.2) | data formatting | bytes 524288
  55.5 0.7 %copy.11 = f32[512,128]{1,0:T(8,128)} copy(f32[512,128]{1,0:T(8,128)S(1)} %get-tuple-element.3) | data formatting | bytes 524288
